TPU v7x, 256 devices: a whole 4x4x8 slice. The times are simulated.
256 devices in a mesh: dp: 16 (over z, core), mp: 16 (over y, x).
Axes of the slice: x: 4, y: 4, z: 8, core: 2. Of those that a mesh axis runs over, the one named last changes fastest.
Arguments:
- activations: bfloat16 [16, 1024, 4096], P('dp'), may hold values from -6 to 6
- out_grads: bfloat16 [16, 1024, 8192], P('dp', None, 'mp'), may hold values from -0.1875 to 0.1875
- error_fb: bfloat16 [16, 4096, 8192], P('dp', None, 'mp'), may hold values from -6 to 6
- q_prev: float32 [8192, 128], P('mp'), may hold values from -0.0625 to 0.0625
Outputs:
- new_error: bfloat16 [16, 4096, 8192], P('dp', None, 'mp')
- q_new: float32 [8192, 128], P('mp')
All inputs are finite; a program needn't handle non-finite values.
Results may differ from a plain program's by a relative error of at most 0.001.
Values sent between devices are 32-bit elements; how exact they have to be, the bound alone decides.
A program may use at most 128 MiB of HBM per device.

v0:
```python
import jax
import jax.numpy as jnp
from jax import lax
from jax.sharding import PartitionSpec as P


def orthonormal(p_part, gram):
    chol = jnp.linalg.cholesky(gram)
    return lax.linalg.triangular_solve(chol, p_part, left_side=False, lower=True, transpose_a=True)


def self_gram(p_part):
    return jnp.dot(p_part.T, p_part, precision=lax.Precision.HIGHEST)


def per_device(activations, out_grads, error_fb, q_prev):
    grad_full = lax.dot_general(
        activations[0], out_grads[0], (((0,), (0,)), ((), ())), preferred_element_type=jnp.float32
    )
    merged = grad_full + error_fb[0].astype(jnp.float32)
    p_local = jnp.dot(merged, q_prev, precision=lax.Precision.HIGHEST)
    p_sum = lax.psum(p_local, ("dp", "mp"))
    p_hat = orthonormal(p_sum, self_gram(p_sum))
    q_local = lax.dot_general(
        merged, p_hat, (((0,), (0,)), ((), ())), precision=lax.Precision.HIGHEST
    )
    q_new = lax.psum(q_local, "dp") / lax.axis_size("dp")
    approx = jnp.dot(p_hat, q_new.T, precision=lax.Precision.HIGHEST)
    new_error = (merged - approx).astype(jnp.bfloat16)[None]
    return (new_error, q_new)


def solution(mesh):
    placed = (P("dp", None, None), P("dp", None, "mp"), P("dp", None, "mp"), P("mp", None))
    return jax.shard_map(
        per_device,
        mesh=mesh,
        in_specs=placed,
        out_specs=(P("dp", None, "mp"), P("mp", None)),
        check_vma=False,
    )
```

profile of v0, /device:TPU:1, one launch (start us, length us, event | category | flops | bytes accessed | tf_op | source)
XLA Modules:
  0.0 475.6 jit_solution(18077918757856505209)
XLA Ops:
  7.2 0.0 copy-start
  7.2 0.0 copy-start.5
  7.2 0.0 all-reduce.3.cloned.1.call-start
  7.2 1.2 copy-done
  8.4 12.1 %convert_add_fusion = f32[4096,512]{1,0:T(8,128)S(1)} fusion(bf16[1,1024,4096]{2,1,0:T(8,128)(2,1)} %param.4, bf16[1,4096,512]{2,1,0:T(8,128)(2,1)} %param.6, bf16[1,1024,512]{2,1,0:T(8,128)(2,1)S(1)} %copy-done), kind=kOutput, calls=%fused_computation | convolution fusion | flops 4299161600 | bytes 22020096 | tf_op jit(solution)/shard_map/dot_general | solution.py:17
  20.5 0.0 copy-start.1
  20.6 3.2 copy-done.1
  23.8 0.0 copy-done.5
  23.8 8.1 %fusion.10 = f32[4096,128]{1,0:T(8,128)} fusion(f32[4096,512]{1,0:T(8,128)S(1)} %convert_add_fusion, f32[512,128]{1,0:T(8,128)S(1)} %copy-done.5), kind=kOutput, calls=%fused_computation.17 | convolution fusion | flops 3221225472 | bytes 10747904 | tf_op jit(solution)/shard_map/dot_general | solution.py:21
  31.8 0.0 all-reduce.3.cloned.1.call-update
  31.9 0.2 all-reduce.5.cloned.1.call-start
  32.1 265.9 %all-reduce.3.cloned.1.call-done = f32[4096,128]{1,0:T(8,128)} async-done(((f32[4096,128]{1,0:T(8,128)}), f32[4096,128]{1,0:T(8,128)}) %all-reduce.3.cloned.1.call-update) | async-done | bytes 2097168 | tf_op jit(solution)/shard_map/psum | solution.py:22
  298.0 0.0 copy-start.2
  298.0 5.8 %fusion.11 = f32[128,128]{1,0:T(8,128)S(1)} fusion(f32[4096,128]{1,0:T(8,128)} %all-reduce.3.cloned.1.call-done), kind=kOutput, calls=%fused_computation.18 | convolution fusion | flops 805306368 | bytes 2162688 | tf_op jit(solution)/shard_map/dot_general | solution.py:13
  303.8 0.1 copy.6
  303.9 11.7 %cholesky.16 = f32[128,128]{1,0:T(8,128)S(1)} custom-call(f32[128,128]{1,0:T(8,128)S(1)} %fusion.9), custom_call_target="Cholesky" | custom-call | tf_op jit(solution)/shard_map/jit(cholesky)/cholesky | solution.py:8
  315.7 0.6 compare_reduce_fusion
  316.3 0.7 fusion.6
  317.0 9.8 %custom-call.6 = f32[1,128,128]{1,2,0:T(8,128)S(1)} custom-call(f32[1,128,128]{2,1,0:T(8,128)S(1)} %fusion.6), custom_call_target="InvertDiagBlocksLowerTriangular" | custom-call | tf_op jit(solution)/shard_map/triangular_solve | solution.py:9
  326.8 0.0 copy-done.2
  326.8 1.8 fusion.7
  328.6 0.0 copy-start.3
  328.6 1.4 copy-done.3
  330.0 16.2 %fusion.12 = f32[512,128]{1,0:T(8,128)} fusion(f32[4096,512]{1,0:T(8,128)} %copy-done.1, f32[4096,128]{1,0:T(8,128)S(1)} %fusion.7), kind=kOutput, calls=%fused_computation.19 | convolution fusion | flops 3221225472 | bytes 10747904 | tf_op jit(solution)/shard_map/dot_general | solution.py:24
  346.1 0.0 all-reduce.5.cloned.1.call-update
  346.2 110.5 %all-reduce.5.cloned.1.call-done = f32[512,128]{1,0:T(8,128)} async-done(((f32[512,128]{1,0:T(8,128)}), f32[512,128]{1,0:T(8,128)}) %all-reduce.5.cloned.1.call-update) | async-done | bytes 262160 | tf_op jit(solution)/shard_map/psum | solution.py:27
  456.7 1.0 broadcast_multiply_fusion
  457.6 0.0 copy-start.4
  457.7 11.2 %fusion.4 = bf16[1,4096,512]{2,1,0:T(8,128)(2,1)} fusion(f32[4096,512]{1,0:T(8,128)} %copy-done.1, f32[4096,128]{1,0:T(8,128)} %copy-done.3, f32[512,128]{1,0:T(8,128)S(1)} %broadcast_multiply_fusion), kind=kOutput, calls=%fused_computation.4 | convolution fusion | flops 3225419776 | bytes 14942208 | tf_op jit(solution)/shard_map/dot_general | solution.py:28
  468.8 0.0 copy-done.4
  (2 shorter events, 0.0 us)
Async XLA Ops:
  7.2 1.2 copy-start
  7.2 16.6 %copy-start.5 = (f32[512,128]{1,0:T(8,128)S(1)}, f32[512,128]{1,0:T(8,128)}, u32[]{:S(2)}) copy-start(f32[512,128]{1,0:T(8,128)} %param.7) | copy-start | bytes 786436
  7.2 290.8 %all-reduce.3.cloned.1.call-start = ((), (), s32[]{:S(2)}) async-start(), calls=%async_computation | async-start | bytes 4194304 | tf_op jit(solution)/shard_map/psum | solution.py:22
  20.5 3.2 copy-start.1
  31.9 424.8 %all-reduce.5.cloned.1.call-start = ((), (), s32[]{:S(2)}) async-start(), calls=%async_computation.1 | async-start | bytes 524288 | tf_op jit(solution)/shard_map/psum | solution.py:27
  298.0 28.8 %copy-start.2 = (f32[4096,128]{1,0:T(8,128)S(1)}, f32[4096,128]{1,0:T(8,128)}, u32[]{:S(2)}) copy-start(f32[4096,128]{1,0:T(8,128)} %all-reduce.3.cloned.1.call-done) | copy-start | bytes 6291460
  328.6 1.4 copy-start.3
  457.6 11.2 %copy-start.4 = (f32[512,128]{1,0:T(8,128)}, f32[512,128]{1,0:T(8,128)S(1)}, u32[]{:S(2)}) copy-start(f32[512,128]{1,0:T(8,128)S(1)} %broadcast_multiply_fusion) | copy-start | bytes 786436
Sparse Core Ops, SparseCore 0:
  32.0 265.9 all-reduce.2
  346.3 110.3 all-reduce.4
where the time goes:
time: 476 us
  waiting for transfers between devices  376 us (79%)
  matrix products  55.1 us (12%)
  other arithmetic  23.8 us (5%)
  between operations  14.1 us (3%)
  local copies, waits for them, and re-layouts  5.86 us (1%)
    psum x1, waiting for transfers between devices, per_device(): p_sum = lax.psum(p_local, ('dp', 'mp'))  266 us
    psum x1, waiting for transfers between devices, per_device(): q_new = lax.psum(q_local, 'dp') / lax.axis_size('dp')  111 us
    dot_general x1, matrix products, per_device(): lax.dot_general(merged, p_hat, (((0,), (0,)), ((), ())), precision=lax.Pr...  16.2 us
    another operation x3, other arithmetic, orthonormal(): chol = jnp.linalg.cholesky(gram)  12.4 us
    dot_general x1, matrix products, per_device(): lax.dot_general(activations[0], out_grads[0], (((0,), (0,)), ((), ())), p...  12.1 us
    dot_general x1, matrix products, per_device(): approx = jnp.dot(p_hat, q_new.T, precision=lax.Precision.HIGHEST)  11.2 us
    another operation x2, other arithmetic, orthonormal(): lax.linalg.triangular_solve(chol, p_part, left_side=False, lower=True, tr...  10.5 us
  transfers between devices with their start and end apart: 2, of which 2 were waited for; matrix products, arithmetic and copies ran while one was open for 0% of the time, Pallas kernels for 0%

commit v1 on v0

--- a/solution.py
+++ b/solution.py
@@ -1,7 +1,221 @@
 import jax
 import jax.numpy as jnp
 from jax import lax
+from jax.experimental import pallas as pl
+from jax.experimental.pallas import tpu as pltpu
 from jax.sharding import PartitionSpec as P
+
+MESH = pl.DeviceIdType.MESH
+NX, NY, NZ = 4, 4, 8
+
+
+def position():
+    dp, mp = lax.axis_index("dp"), lax.axis_index("mp")
+    return lax.rem(mp, NX), mp // NX, dp // 2, lax.rem(dp, 2)
+
+
+def device(x, y, z, c):
+    return (z * 2 + c, y * NX + x)
+
+
+def remote(src, dst, send, recv, where):
+    return pltpu.make_async_remote_copy(
+        src_ref=src, dst_ref=dst, send_sem=send, recv_sem=recv, device_id=where, device_id_type=MESH
+    )
+
+
+def drain(like, sem):
+    pltpu.make_async_copy(like, like, sem).wait()
+
+
+def loop(count, body):
+    def step(k, carry):
+        body(k)
+        return carry
+
+    lax.fori_loop(0, count, step, 0)
+
+
+def sum_p_kernel(p, out, h, r0, r1, u, r2, v, r3, send, got0, got1, got2, got3, bak3, bak2, bak1, bak0):
+    x, y, z, c = position()
+    partner = device(x, y, z, 1 - c)
+    turn = lambda own, d, n: lax.rem(own + d, n)
+    xs = [device(turn(x, d, NX), y, z, c) for d in range(1, NX)]
+    ys = [device(x, turn(y, d, NY), z, c) for d in range(1, NY)]
+    zs = [device(x, y, turn(z, d, NZ), c) for d in range(1, NZ)]
+    barrier = pltpu.get_barrier_semaphore()
+    for peer in [partner] + xs + ys + zs:
+        pl.semaphore_signal(barrier, inc=1, device_id=peer, device_id_type=MESH)
+    pl.semaphore_wait(barrier, 1 + len(xs) + len(ys) + len(zs))
+
+    def pair_out(k):
+        remote(p.at[k, 1 - c], r0.at[k], send.at[0], got0.at[k], partner).start()
+
+    loop(NZ, pair_out)
+
+    def first(k):
+        drain(r0.at[k], got0.at[k])
+        h[k] = p[k, c] + r0[k]
+        for d in range(1, NX):
+            remote(h.at[k, 0, turn(x, d, NX)], r1.at[k, 0, d - 1], send.at[1], got1.at[k], xs[d - 1]).start()
+            remote(h.at[k, 1, turn(y, d, NY)], r1.at[k, 1, d - 1], send.at[1], got1.at[k], ys[d - 1]).start()
+
+    loop(NZ, first)
+
+    def second(k):
+        drain(r1.at[k], got1.at[k])
+        for part, own in ((0, x), (1, y)):
+            u[k, part] = h[k, part, own] + r1[k, part, 0] + r1[k, part, 1] + r1[k, part, 2]
+        for d in range(1, NX):
+            remote(u.at[k, 0, turn(y, d, NY)], r2.at[k, 0, d - 1], send.at[2], got2.at[k], ys[d - 1]).start()
+            remote(u.at[k, 1, turn(x, d, NX)], r2.at[k, 1, d - 1], send.at[2], got2.at[k], xs[d - 1]).start()
+
+    loop(NZ, second)
+
+    def third(k):
+        drain(r2.at[k], got2.at[k])
+        for part, own in ((0, y), (1, x)):
+            v[k, part] = u[k, part, own] + r2[k, part, 0] + r2[k, part, 1] + r2[k, part, 2]
+
+        @pl.when(k != z)
+        def _():
+            remote(v.at[k], r3.at[lax.rem(z - k + NZ, NZ) - 1], send.at[3], got3, device(x, y, k, c)).start()
+
+    loop(NZ, third)
+    drain(r3, got3)
+    total = v[z]
+    for d in range(NZ - 1):
+        total = total + r3[d]
+    out[z, c, 0, x, y] = total[0]
+    out[z, c, 1, y, x] = total[1]
+    for d in range(1, NZ):
+        for piece in (out.at[z, c, 0, x, y], out.at[z, c, 1, y, x]):
+            remote(piece, piece, send.at[4], bak3.at[z], zs[d - 1]).start()
+
+    def third_back(i):
+        k = lax.rem(z + i, NZ)
+
+        @pl.when(i != 0)
+        def _():
+            drain(v.at[k], bak3.at[k])
+
+        for d in range(1, NX):
+            a, b = out.at[k, c, 0, x, y], out.at[k, c, 1, y, x]
+            remote(a, a, send.at[5], bak2.at[k], ys[d - 1]).start()
+            remote(b, b, send.at[5], bak2.at[k], xs[d - 1]).start()
+
+    loop(NZ, third_back)
+
+    def second_back(i):
+        k = lax.rem(z + i, NZ)
+        drain(r2.at[k], bak2.at[k])
+        for d in range(1, NX):
+            a, b = out.at[k, c, 0, x], out.at[k, c, 1, y]
+            remote(a, a, send.at[6], bak1.at[k], xs[d - 1]).start()
+            remote(b, b, send.at[6], bak1.at[k], ys[d - 1]).start()
+
+    loop(NZ, second_back)
+
+    def first_back(i):
+        k = lax.rem(z + i, NZ)
+        drain(r1.at[k], bak1.at[k])
+        remote(out.at[k, c], out.at[k, c], send.at[7], bak0.at[k], partner).start()
+
+    loop(NZ, first_back)
+
+    def pair_back(k):
+        drain(r0.at[k], bak0.at[k])
+
+    loop(NZ, pair_back)
+    drain(r0, send.at[0])
+    drain(r1, send.at[1])
+    drain(r2, send.at[2])
+    drain(r3, send.at[3])
+    drain(r3, send.at[4])
+    drain(r2, send.at[5])
+    drain(r1, send.at[6])
+    drain(r0, send.at[7])
+
+
+def sum_p(p):
+    shape = (NZ, 2, 2, NX, NY, 8, 128)
+    f32 = lambda *dims: pltpu.VMEM(dims + (8, 128), jnp.float32)
+    sem = pltpu.SemaphoreType.DMA
+    out = pl.pallas_call(
+        sum_p_kernel,
+        out_shape=jax.ShapeDtypeStruct(shape, jnp.float32),
+        in_specs=[pl.BlockSpec(memory_space=pltpu.VMEM)],
+        out_specs=pl.BlockSpec(memory_space=pltpu.VMEM),
+        scratch_shapes=[
+            f32(NZ, 2, NX, NY),
+            f32(NZ, 2, NX, NY),
+            f32(NZ, 2, NX - 1, NY),
+            f32(NZ, 2, NY),
+            f32(NZ, 2, NY - 1),
+            f32(NZ, 2),
+            f32(NZ - 1, 2),
+            sem((8,)),
+            sem((NZ,)),
+            sem((NZ,)),
+            sem((NZ,)),
+            sem(()),
+            sem((NZ,)),
+            sem((NZ,)),
+            sem((NZ,)),
+            sem((NZ,)),
+        ],
+        compiler_params=pltpu.CompilerParams(collective_id=0, has_side_effects=True),
+    )(p.reshape(shape))
+    return out.reshape(4096, 128)
+
+
+def sum_s_kernel(s, out, h, r0, r1, w, send, got0, got1, bak1, bak0):
+    x, y, z, c = position()
+    partner = device(x, y, z, 1 - c)
+    zs = [device(x, y, lax.rem(z + d, NZ), c) for d in range(1, NZ)]
+    barrier = pltpu.get_barrier_semaphore()
+    for peer in [partner] + zs:
+        pl.semaphore_signal(barrier, inc=1, device_id=peer, device_id_type=MESH)
+    pl.semaphore_wait(barrier, 1 + len(zs))
+    remote(s.at[1 - c], r0, send.at[0], got0, partner).start()
+    drain(r0, got0)
+    h[...] = s[c] + r0[...]
+    for d in range(1, NZ):
+        remote(h.at[lax.rem(z + d, NZ)], r1.at[d - 1], send.at[1], got1, zs[d - 1]).start()
+    drain(r1, got1)
+    total = h[z]
+    for d in range(NZ - 1):
+        total = total + r1[d]
+    w[...] = total
+    out[c, z] = total
+    for d in range(1, NZ):
+        remote(w, out.at[c, z], send.at[2], bak1.at[z], zs[d - 1]).start()
+    remote(w, out.at[c, z], send.at[3], bak0.at[z], partner).start()
+    for d in range(1, NZ):
+        k = lax.rem(z + d, NZ)
+        drain(w, bak1.at[k])
+        remote(out.at[c, k], out.at[c, k], send.at[3], bak0.at[k], partner).start()
+    for k in range(NZ):
+        drain(w, bak0.at[k])
+    drain(r0, send.at[0])
+    drain(r1, send.at[1])
+    drain(r1, send.at[2])
+    drain(r0, send.at[3])
+
+
+def sum_s(s):
+    shape = (2, NZ, 8, 512)
+    f32 = lambda *dims: pltpu.VMEM(dims + (8, 512), jnp.float32)
+    sem = pltpu.SemaphoreType.DMA
+    out = pl.pallas_call(
+        sum_s_kernel,
+        out_shape=jax.ShapeDtypeStruct(shape, jnp.float32),
+        in_specs=[pl.BlockSpec(memory_space=pltpu.VMEM)],
+        out_specs=pl.BlockSpec(memory_space=pltpu.VMEM),
+        scratch_shapes=[f32(NZ), f32(NZ), f32(NZ - 1), f32(), sem((4,)), sem(()), sem(()), sem((NZ,)), sem((NZ,))],
+        compiler_params=pltpu.CompilerParams(collective_id=1, has_side_effects=True),
+    )(s.reshape(shape))
+    return out.reshape(128, 512)
 
 
 def orthonormal(p_part, gram):
@@ -19,15 +233,15 @@
     )
     merged = grad_full + error_fb[0].astype(jnp.float32)
     p_local = jnp.dot(merged, q_prev, precision=lax.Precision.HIGHEST)
-    p_sum = lax.psum(p_local, ("dp", "mp"))
+    p_sum = sum_p(p_local)
     p_hat = orthonormal(p_sum, self_gram(p_sum))
-    q_local = lax.dot_general(
-        merged, p_hat, (((0,), (0,)), ((), ())), precision=lax.Precision.HIGHEST
-    )
-    q_new = lax.psum(q_local, "dp") / lax.axis_size("dp")
-    approx = jnp.dot(p_hat, q_new.T, precision=lax.Precision.HIGHEST)
+    q_local_t = lax.dot_general(
+        p_hat, merged, (((0,), (0,)), ((), ())), precision=lax.Precision.HIGHEST
+    )
+    q_new_t = sum_s(q_local_t) / lax.axis_size("dp")
+    approx = jnp.dot(p_hat, q_new_t, precision=lax.Precision.HIGHEST)
     new_error = (merged - approx).astype(jnp.bfloat16)[None]
-    return (new_error, q_new)
+    return (new_error, q_new_t.T)
 
 
 def solution(mesh):

time: 476 us -> 138 us (0.29)
  waiting for transfers between devices: 376 us -> 0 us
  Pallas kernels: 0 us -> 63 us
  between operations: 14.1 us -> 0.74 us
  matrix products: 55.1 us -> 48.2 us
    psum x2 -> x0, waiting for transfers between devices: 376 us -> none  [the longest x1 266 us: per_device(): p_sum = lax.psum(p_local, ('dp', 'mp'))]
    pallas_call x0 -> x2, Pallas kernels: none -> 63 us  [the longest x1 44.7 us: sum_p(): pl.pallas_call(sum_p_kernel, out_shape=jax.ShapeDtypeStruct(shape, jnp.fl...]
    dot_general x2, matrix products: 27.3 us -> 18.9 us  [the longest x1 10.5 us: per_device(): approx = jnp.dot(p_hat, q_new_t, precision=lax.Precision.HIGHEST)]
  transfers between devices with their start and end apart: 2 -> 0, of which waited for: 2 -> 0; matrix products, arithmetic and copies ran while one was open for 0% -> 0% of each run, Pallas kernels for 0% -> 0%
where the time goes in v1:
time: 138 us
  Pallas kernels  63 us (46%)
  matrix products  48.2 us (35%)
  other arithmetic  23.8 us (17%)
  local copies, waits for them, and re-layouts  2.14 us (2%)
    pallas_call x1, Pallas kernels, sum_p(): pl.pallas_call(sum_p_kernel, out_shape=jax.ShapeDtypeStruct(shape, jnp.fl...  44.7 us
    pallas_call x1, Pallas kernels, sum_s(): pl.pallas_call(sum_s_kernel, out_shape=jax.ShapeDtypeStruct(shape, jnp.fl...  18.4 us
    another operation x3, other arithmetic, orthonormal(): chol = jnp.linalg.cholesky(gram)  12.4 us
    dot_general x1, matrix products, per_device(): lax.dot_general(activations[0], out_grads[0], (((0,), (0,)), ((), ())), p...  12.1 us
    dot_general x1, matrix products, per_device(): approx = jnp.dot(p_hat, q_new_t, precision=lax.Precision.HIGHEST)  10.5 us
    another operation x2, other arithmetic, orthonormal(): lax.linalg.triangular_solve(chol, p_part, left_side=False, lower=True, tr...  10.5 us
    dot_general x1, matrix products, per_device(): lax.dot_general(p_hat, merged, (((0,), (0,)), ((), ())), precision=lax.Pr...  8.34 us
    dot_general x1, matrix products, per_device(): p_local = jnp.dot(merged, q_prev, precision=lax.Precision.HIGHEST)  8.07 us

profile of v1, /device:TPU:1, one launch (start us, length us, event | category | flops | bytes accessed | tf_op | source)
XLA Modules:
  0.0 137.9 jit_solution(3758453839991857288)
XLA Ops:
  0.6 0.0 copy-start
  0.6 0.0 copy-start.2
  0.7 1.2 copy-done
  1.9 12.1 %convert_add_fusion = f32[4096,512]{1,0:T(8,128)S(1)} fusion(bf16[1,1024,4096]{2,1,0:T(8,128)(2,1)} %param.4, bf16[1,4096,512]{2,1,0:T(8,128)(2,1)} %param.6, bf16[1,1024,512]{2,1,0:T(8,128)(2,1)S(1)} %copy-done), kind=kOutput, calls=%fused_computation | convolution fusion | flops 4299161600 | bytes 22020096 | tf_op jit(solution)/shard_map/dot_general | solution.py:231
  14.0 0.0 copy-done.2
  14.0 0.0 copy-start.1
  14.0 8.1 %fusion.10 = f32[4096,128]{1,0:T(8,128)} fusion(f32[4096,512]{1,0:T(8,128)S(1)} %convert_add_fusion, f32[512,128]{1,0:T(8,128)S(1)} %copy-done.2), kind=kOutput, calls=%fused_computation.18 | convolution fusion | flops 3221225472 | bytes 10747904 | tf_op jit(solution)/shard_map/dot_general | solution.py:235
  22.1 0.0 copy-done.1
  22.1 44.7 %shard_map.59 = f32[8,2,2,4,4,8,128]{6,5,4,3,2,1,0:T(8,128)} custom-call(f32[8,2,2,4,4,8,128]{6,5,4,3,2,1,0:T(8,128)} %bitcast.40), custom_call_target="tpu_custom_call" | custom-call | tf_op jit(solution)/shard_map/pallas_call | solution.py:144
  66.8 5.7 %convolution_bitcast_fusion = f32[128,128]{1,0:T(8,128)S(1)} fusion(f32[8,2,2,4,4,8,128]{6,5,4,3,2,1,0:T(8,128)} %shard_map.59), kind=kOutput, calls=%fused_computation.5 | convolution fusion | flops 805306368 | bytes 2162688 | tf_op jit(solution)/shard_map/dot_general | solution.py:227
  72.5 0.1 copy.6
  72.6 11.7 %cholesky.16 = f32[128,128]{1,0:T(8,128)S(1)} custom-call(f32[128,128]{1,0:T(8,128)S(1)} %fusion.9), custom_call_target="Cholesky" | custom-call | tf_op jit(solution)/shard_map/jit(cholesky)/cholesky | solution.py:222
  84.4 0.6 compare_reduce_fusion
  85.0 0.7 fusion.6
  85.7 9.8 %custom-call.6 = f32[1,128,128]{1,2,0:T(8,128)S(1)} custom-call(f32[1,128,128]{2,1,0:T(8,128)S(1)} %fusion.6), custom_call_target="InvertDiagBlocksLowerTriangular" | custom-call | tf_op jit(solution)/shard_map/triangular_solve | solution.py:223
  95.5 3.4 %fusion.7 = f32[4096,128]{1,0:T(8,128)S(1)} fusion(f32[4096,128]{1,0:T(8,128)} %bitcast.41, f32[1,128,128]{1,2,0:T(8,128)S(1)} %custom-call.6), kind=kOutput, calls=%fused_computation.10 | convolution fusion | flops 805306368 | bytes 4259840 | tf_op jit(solution)/shard_map/triangular_solve | solution.py:223
  98.9 8.3 %fusion.11 = f32[128,512]{1,0:T(8,128)} fusion(f32[4096,128]{1,0:T(8,128)S(1)} %fusion.7, f32[4096,512]{1,0:T(8,128)} %copy-done.1), kind=kOutput, calls=%fused_computation.19 | convolution fusion | flops 3221225472 | bytes 10747904 | tf_op jit(solution)/shard_map/dot_general | solution.py:238
  107.2 18.4 %shard_map.60 = f32[2,8,8,512]{3,2,1,0:T(8,128)} custom-call(f32[2,8,8,512]{3,2,1,0:T(8,128)} %bitcast.44), custom_call_target="tpu_custom_call" | custom-call | tf_op jit(solution)/shard_map/pallas_call | solution.py:210
  125.6 1.0 broadcast_multiply_fusion
  126.6 10.5 %fusion.4 = bf16[1,4096,512]{2,1,0:T(8,128)(2,1)} fusion(f32[4096,512]{1,0:T(8,128)} %copy-done.1, f32[4096,128]{1,0:T(8,128)S(1)} %fusion.7, f32[128,512]{1,0:T(8,128)S(1)} %bitcast.42), kind=kOutput, calls=%fused_computation.4 | convolution fusion | flops 3225419776 | bytes 14942208 | tf_op jit(solution)/shard_map/dot_general | solution.py:242
  137.1 0.8 copy.7
  (2 shorter events, 0.0 us)
Async XLA Ops:
  0.6 1.2 copy-start
  0.6 13.4 %copy-start.2 = (f32[512,128]{1,0:T(8,128)S(1)}, f32[512,128]{1,0:T(8,128)}, u32[]{:S(2)}) copy-start(f32[512,128]{1,0:T(8,128)} %param.7) | copy-start | bytes 786436
  14.0 8.1 %copy-start.1 = (f32[4096,512]{1,0:T(8,128)}, f32[4096,512]{1,0:T(8,128)S(1)}, u32[]{:S(2)}) copy-start(f32[4096,512]{1,0:T(8,128)S(1)} %convert_add_fusion) | copy-start | bytes 25165828

commit v2 on v0

v2 whole, which is shorter than its diff:
```python
import jax
import jax.numpy as jnp
from jax import lax
from jax.experimental import pallas as pl
from jax.experimental.pallas import tpu as pltpu
from jax.sharding import PartitionSpec as P

MESH = pl.DeviceIdType.MESH
NX, NY, NZ = 4, 4, 8
TOK, ROWS, COLS, RANK = 1024, 4096, 512, 128
CHUNK = ROWS // NZ
BLOCK = 16
BF, F32 = jnp.bfloat16, jnp.float32
HIGHEST = lax.Precision.HIGHEST
FIRST = (((0,), (0,)), ((), ()))


def position():
    dp, mp = lax.axis_index("dp"), lax.axis_index("mp")
    return lax.rem(mp, NX), mp // NX, dp // 2, lax.rem(dp, 2)


def device(x, y, z, c):
    return (z * 2 + c, y * NX + x)


def turn(own, d, n):
    return lax.rem(own + d, n)


def remote(src, dst, send, recv, where):
    return pltpu.make_async_remote_copy(
        src_ref=src, dst_ref=dst, send_sem=send, recv_sem=recv, device_id=where, device_id_type=MESH
    )


def drain(like, sem):
    pltpu.make_async_copy(like, like, sem).wait()


def loop(first, last, body):
    def step(k, carry):
        body(k)
        return carry

    lax.fori_loop(first, last, step, 0)


def halves(value):
    high = value.astype(BF)
    return high, (value - high.astype(F32)).astype(BF)


def dot(a, b, dims=(((1,), (0,)), ((), ()))):
    return lax.dot_general(a, b, dims, preferred_element_type=F32)


def eliminate(m, b):
    at = b * BLOCK
    block = m[at : at + BLOCK, :]
    row = lax.broadcasted_iota(jnp.int32, (BLOCK, 1), 0)
    for j in range(BLOCK):
        scale = lax.rsqrt(block[j : j + 1, at + j : at + j + 1])
        pivot = block[j : j + 1, :] * scale
        factor = block[:, at + j : at + j + 1] * scale
        block = jnp.where(row == j, pivot, jnp.where(row > j, block - factor * pivot, block))
    m[at : at + BLOCK, :] = block
    if at + BLOCK < RANK:
        update = lax.dot_general(block[:, :RANK], block, FIRST, precision=HIGHEST, preferred_element_type=F32)
        m[at + BLOCK :, :] -= update[at + BLOCK :, :]


def step_kernel(
    a, g, e, q,
    hi_out, lo_out, p_out, w_out, q_out,
    abuf, ebuf, gbuf, hi, lo, qcat, p, h, r0, r1, u, r2, v, r3, full, both,
    acc, sq, cross, m, s, s0, hs, s1, sw, sall,
    asem, esem, gsem, osem, send, got0, got1, got2, got3, bak3, bak2, bak1, bak0,
    ssend, sgot0, sgot1, sbak1, sbak0,
):
    x, y, z, c = position()
    partner = device(x, y, z, 1 - c)
    xs = [device(turn(x, d, NX), y, z, c) for d in range(1, NX)]
    ys = [device(x, turn(y, d, NY), z, c) for d in range(1, NY)]
    zs = [device(x, y, turn(z, d, NZ), c) for d in range(1, NZ)]
    rows = lambda k: pl.ds(pl.multiple_of(k * CHUNK, CHUNK), CHUNK)

    def loads(k, slot):
        return (
            pltpu.make_async_copy(a.at[:, rows(k)], abuf.at[slot], asem.at[slot]),
            pltpu.make_async_copy(e.at[rows(k)], ebuf.at[slot], esem.at[slot]),
        )

    whole_g = pltpu.make_async_copy(g, gbuf, gsem)
    whole_g.start()
    for copy in loads(0, 0):
        copy.start()
    barrier = pltpu.get_barrier_semaphore()
    for peer in [partner] + xs + ys + zs:
        pl.semaphore_signal(barrier, inc=1, device_id=peer, device_id_type=MESH)
    q_high, q_low = halves(q[...])
    qcat[:, :RANK] = q_high
    qcat[:, RANK:] = q_low
    acc[...] = jnp.zeros_like(acc)
    sq[...] = jnp.zeros_like(sq)
    cross[...] = jnp.zeros_like(cross)
    whole_g.wait()

    def compute(k):
        slot = lax.rem(k, 2)

        @pl.when(k < NZ - 1)
        def _():
            for copy in loads(k + 1, 1 - slot):
                copy.start()

        for copy in loads(k, slot):
            copy.wait()
        merged = dot(abuf[slot], gbuf[...], FIRST) + ebuf[slot].astype(F32)
        high, low = halves(merged)
        hi[rows(k)] = high
        lo[rows(k)] = low
        wide = dot(high, qcat[...])
        part = wide[:, :RANK] + wide[:, RANK:] + dot(low, qcat[:, :RANK])
        p[k] = part.reshape(2, 2, NX, NY, 8, RANK)
        pltpu.make_async_copy(hi.at[rows(k)], hi_out.at[rows(k)], osem.at[0]).start()
        pltpu.make_async_copy(lo.at[rows(k)], lo_out.at[rows(k)], osem.at[1]).start()

    def pair(k):
        remote(p.at[k, 1 - c], r0.at[k], send.at[0], got0.at[k], partner).start()

    def first(k):
        drain(r0.at[k], got0.at[k])
        h[k] = p[k, c] + r0[k]
        for d in range(1, NX):
            remote(h.at[k, 0, turn(x, d, NX)], r1.at[k, 0, d - 1], send.at[1], got1.at[k], xs[d - 1]).start()
            remote(h.at[k, 1, turn(y, d, NY)], r1.at[k, 1, d - 1], send.at[1], got1.at[k], ys[d - 1]).start()

    def second(k):
        drain(r1.at[k], got1.at[k])
        for part, own in ((0, x), (1, y)):
            u[k, part] = h[k, part, own] + r1[k, part, 0] + r1[k, part, 1] + r1[k, part, 2]
        for d in range(1, NX):
            remote(u.at[k, 0, turn(y, d, NY)], r2.at[k, 0, d - 1], send.at[2], got2.at[k], ys[d - 1]).start()
            remote(u.at[k, 1, turn(x, d, NX)], r2.at[k, 1, d - 1], send.at[2], got2.at[k], xs[d - 1]).start()

    def third(k):
        drain(r2.at[k], got2.at[k])
        for part, own in ((0, y), (1, x)):
            v[k, part] = u[k, part, own] + r2[k, part, 0] + r2[k, part, 1] + r2[k, part, 2]

        @pl.when(k != z)
        def _():
            remote(v.at[k], r3.at[lax.rem(z - k + NZ, NZ) - 1], send.at[3], got3, device(x, y, k, c)).start()

    pl.semaphore_wait(barrier, 1 + len(xs) + len(ys) + len(zs))
    lag1, lag2, lag3 = 1, 4, 6

    def forward(k):
        compute(k)
        pair(k)

        @pl.when(k >= lag1)
        def _():
            first(k - lag1)

        @pl.when(k >= lag2)
        def _():
            second(k - lag2)

        @pl.when(k >= lag3)
        def _():
            third(k - lag3)

    loop(0, NZ, forward)
    loop(NZ - lag1, NZ, first)
    loop(NZ - lag2, NZ, second)
    loop(NZ - lag3, NZ, third)
    drain(r3, got3)
    total = v[z]
    for d in range(NZ - 1):
        total = total + r3[d]
    full[z, c, 0, x, y] = total[0]
    full[z, c, 1, y, x] = total[1]
    for d in range(1, NZ):
        for piece in (full.at[z, c, 0, x, y], full.at[z, c, 1, y, x]):
            remote(piece, piece, send.at[4], bak3.at[z], zs[d - 1]).start()

    def third_back(i):
        k = turn(z, i, NZ)

        @pl.when(i != 0)
        def _():
            drain(v.at[k], bak3.at[k])

        for d in range(1, NX):
            one, two = full.at[k, c, 0, x, y], full.at[k, c, 1, y, x]
            remote(one, one, send.at[5], bak2.at[k], ys[d - 1]).start()
            remote(two, two, send.at[5], bak2.at[k], xs[d - 1]).start()

    def second_back(i):
        k = turn(z, i, NZ)
        drain(r2.at[k], bak2.at[k])
        for d in range(1, NX):
            one, two = full.at[k, c, 0, x], full.at[k, c, 1, y]
            remote(one, one, send.at[6], bak1.at[k], xs[d - 1]).start()
            remote(two, two, send.at[6], bak1.at[k], ys[d - 1]).start()

    def first_back(i):
        k = turn(z, i, NZ)
        drain(r1.at[k], bak1.at[k])
        remote(full.at[k, c], full.at[k, c], send.at[7], bak0.at[k], partner).start()

    def use(i):
        k = turn(z, i, NZ)
        drain(r0.at[k], bak0.at[k])
        block = full[k].reshape(CHUNK, RANK)
        high, low = halves(block)
        rest = ((block - high.astype(F32)) - low.astype(F32)).astype(BF)
        both[rows(k), :RANK] = high
        both[rows(k), RANK:] = low
        pltpu.make_async_copy(both.at[rows(k)], p_out.at[rows(k)], osem.at[2]).start()
        pair_ = both[rows(k)]
        acc[...] += dot(pair_, hi[rows(k)], FIRST)
        acc[:RANK] += dot(high, lo[rows(k)], FIRST)
        sq[...] += dot(pair_, pair_, FIRST)
        cross[...] += dot(high, rest, FIRST)

    loop(0, NZ, third_back)
    loop(0, NZ, second_back)

    def backward(i):
        first_back(i)

        @pl.when(i >= 1)
        def _():
            use(i - 1)

    loop(0, NZ, backward)
    use(NZ - 1)

    s[...] = (acc[:RANK] + acc[RANK:]).reshape(2, NZ, 8, COLS)
    remote(s.at[1 - c], s0, ssend.at[0], sgot0, partner).start()
    mixed = sq[:RANK, RANK:] + cross[...]
    m[:, :RANK] = sq[:RANK, :RANK] + (sq[RANK:, RANK:] + (mixed + mixed.T))
    diagonal = lax.broadcasted_iota(jnp.int32, (RANK, RANK), 0) == lax.broadcasted_iota(jnp.int32, (RANK, RANK), 1)
    m[:, RANK:] = diagonal.astype(F32)
    eliminate(m, 0)
    drain(s0, sgot0)
    hs[...] = s[c] + s0[...]
    for d in range(1, NZ):
        remote(hs.at[turn(z, d, NZ)], s1.at[d - 1], ssend.at[1], sgot1, zs[d - 1]).start()
    for b in (1, 2, 3, 4):
        eliminate(m, b)
    drain(s1, sgot1)
    total = hs[z]
    for d in range(NZ - 1):
        total = total + s1[d]
    sw[...] = total
    sall[c, z] = total
    for d in range(1, NZ):
        remote(sw, sall.at[c, z], ssend.at[2], sbak1.at[z], zs[d - 1]).start()
    remote(sw, sall.at[c, z], ssend.at[3], sbak0.at[z], partner).start()
    for b in (5, 6, 7):
        eliminate(m, b)

    def relay(i):
        k = turn(z, i, NZ)
        drain(sw, sbak1.at[k])
        remote(sall.at[c, k], sall.at[c, k], ssend.at[3], sbak0.at[k], partner).start()

    loop(1, NZ, relay)

    def arrive(k):
        drain(sw, sbak0.at[k])

    loop(0, NZ, arrive)
    inverse = m[:, RANK:]
    scaled = sall[...].reshape(RANK, COLS) * (1.0 / (2 * NZ))
    q_new = jnp.dot(inverse, scaled, precision=HIGHEST, preferred_element_type=F32)
    q_out[...] = q_new
    w_out[...] = lax.dot_general(inverse, q_new, FIRST, precision=HIGHEST, preferred_element_type=F32)

    drain(r0, send.at[0])
    drain(r1, send.at[1])
    drain(r2, send.at[2])
    drain(r3, send.at[3])
    drain(r3, send.at[4])
    drain(r2, send.at[5])
    drain(r1, send.at[6])
    drain(r0, send.at[7])
    drain(s0, ssend.at[0])
    drain(s1, ssend.at[1])
    drain(s1, ssend.at[2])
    drain(s0, ssend.at[3])
    pltpu.make_async_copy(hi, hi_out, osem.at[0]).wait()
    pltpu.make_async_copy(lo, lo_out, osem.at[1]).wait()
    pltpu.make_async_copy(both, p_out, osem.at[2]).wait()


def step(activations, out_grads, error_fb, q_prev):
    anywhere = pl.BlockSpec(memory_space=pl.ANY)
    near = pl.BlockSpec(memory_space=pltpu.VMEM)
    vm = lambda *dims: pltpu.VMEM(dims, F32)
    bf = lambda *dims: pltpu.VMEM(dims, BF)
    sem = lambda *dims: pltpu.SemaphoreType.DMA(dims)
    return pl.pallas_call(
        step_kernel,
        out_shape=[
            jax.ShapeDtypeStruct((ROWS, COLS), BF),
            jax.ShapeDtypeStruct((ROWS, COLS), BF),
            jax.ShapeDtypeStruct((ROWS, 2 * RANK), BF),
            jax.ShapeDtypeStruct((RANK, COLS), F32),
            jax.ShapeDtypeStruct((RANK, COLS), F32),
        ],
        in_specs=[anywhere, anywhere, anywhere, near],
        out_specs=[anywhere, anywhere, anywhere, near, near],
        scratch_shapes=[
            bf(2, TOK, CHUNK),
            bf(2, CHUNK, COLS),
            bf(TOK, COLS),
            bf(ROWS, COLS),
            bf(ROWS, COLS),
            bf(COLS, 2 * RANK),
            vm(NZ, 2, 2, NX, NY, 8, RANK),
            vm(NZ, 2, NX, NY, 8, RANK),
            vm(NZ, 2, NX, NY, 8, RANK),
            vm(NZ, 2, NX - 1, NY, 8, RANK),
            vm(NZ, 2, NY, 8, RANK),
            vm(NZ, 2, NY - 1, 8, RANK),
            vm(NZ, 2, 8, RANK),
            vm(NZ - 1, 2, 8, RANK),
            vm(NZ, 2, 2, NX, NY, 8, RANK),
            bf(ROWS, 2 * RANK),
            vm(2 * RANK, COLS),
            vm(2 * RANK, 2 * RANK),
            vm(RANK, RANK),
            vm(RANK, 2 * RANK),
            vm(2, NZ, 8, COLS),
            vm(NZ, 8, COLS),
            vm(NZ, 8, COLS),
            vm(NZ - 1, 8, COLS),
            vm(8, COLS),
            vm(2, NZ, 8, COLS),
            sem(2),
            sem(2),
            sem(),
            sem(3),
            sem(8),
            sem(NZ),
            sem(NZ),
            sem(NZ),
            sem(),
            sem(NZ),
            sem(NZ),
            sem(NZ),
            sem(NZ),
            sem(4),
            sem(),
            sem(),
            sem(NZ),
            sem(NZ),
        ],
        compiler_params=pltpu.CompilerParams(
            collective_id=0, has_side_effects=True, vmem_limit_bytes=40 << 20
        ),
        name="step",
    )(activations, out_grads, error_fb, q_prev)


def finish_kernel(p, w, q_t, hi, lo, out, q_new):
    @pl.when(pl.program_id(0) == 0)
    def _():
        q_new[...] = q_t[...].T

    high, low = halves(w[...])
    approx = dot(p[...], jnp.concatenate([high, high], axis=0)) + dot(p[:, :RANK], low)
    out[...] = ((hi[...].astype(F32) - approx) + lo[...].astype(F32)).astype(BF)


def finish(p, w, q_t, hi, lo):
    tile = 1024
    fixed = lambda *dims: pl.BlockSpec(dims, lambda i: (0, 0))
    moving = lambda *dims: pl.BlockSpec(dims, lambda i: (i, 0))
    return pl.pallas_call(
        finish_kernel,
        out_shape=[jax.ShapeDtypeStruct((ROWS, COLS), BF), jax.ShapeDtypeStruct((COLS, RANK), F32)],
        grid=(ROWS // tile,),
        in_specs=[
            moving(tile, 2 * RANK), fixed(RANK, COLS), fixed(RANK, COLS), moving(tile, COLS), moving(tile, COLS)
        ],
        out_specs=[moving(tile, COLS), fixed(COLS, RANK)],
        compiler_params=pltpu.CompilerParams(vmem_limit_bytes=24 << 20),
        name="finish",
    )(p, w, q_t, hi, lo)


def per_device(activations, out_grads, error_fb, q_prev):
    hi, lo, p, w, q_t = step(activations[0], out_grads[0], error_fb[0], q_prev)
    new_error, q_new = finish(p, w, q_t, hi, lo)
    return (new_error[None], q_new)


def solution(mesh):
    placed = (P("dp", None, None), P("dp", None, "mp"), P("dp", None, "mp"), P("mp", None))
    return jax.shard_map(
        per_device,
        mesh=mesh,
        in_specs=placed,
        out_specs=(P("dp", None, "mp"), P("mp", None)),
        check_vma=False,
    )
```

time: 476 us -> 75.3 us (0.16)
  waiting for transfers between devices: 376 us -> 0 us
  Pallas kernels: 0 us -> 72.2 us
  matrix products: 55.1 us -> 0 us
  other arithmetic: 23.8 us -> 0 us
  between operations: 14.1 us -> 0.65 us
    psum x2 -> x0, waiting for transfers between devices: 376 us -> none  [the longest x1 266 us: per_device(): p_sum = lax.psum(p_local, ('dp', 'mp'))]
    pallas_call x0 -> x2, Pallas kernels: none -> 72.2 us  [the longest x1 67.7 us: step(): pl.pallas_call(step_kernel, out_shape=[jax.ShapeDtypeStruct((ROWS, COLS),...]
    dot_general x5 -> x0, matrix products: 53.3 us -> none  [the longest x1 16.2 us: per_device(): lax.dot_general(merged, p_hat, (((0,), (0,)), ((), ())), precision=lax.Pr...]
    another operation x5 -> x0, other arithmetic: 22.9 us -> none  [the longest x3 12.4 us: orthonormal(): chol = jnp.linalg.cholesky(gram)]
  transfers between devices with their start and end apart: 2 -> 0, of which waited for: 2 -> 0; matrix products, arithmetic and copies ran while one was open for 0% -> 0% of each run, Pallas kernels for 0% -> 0%
where the time goes in v2:
time: 75.3 us; the launch traced here: 75 us
  Pallas kernels  72.2 us (96%)
  local copies, waits for them, and re-layouts  2.17 us (3%)
    pallas_call x1, Pallas kernels, step(): pl.pallas_call(step_kernel, out_shape=[jax.ShapeDtypeStruct((ROWS, COLS),...  67.7 us
    pallas_call x1, Pallas kernels, finish(): pl.pallas_call(finish_kernel, out_shape=[jax.ShapeDtypeStruct((ROWS, COLS...  4.46 us
    unnamed x4, local copies, waits for them, and re-layouts  2.17 us

profile of v2, /device:TPU:1, one launch (start us, length us, event | category | flops | bytes accessed | tf_op | source)
XLA Modules:
  0.0 75.0 jit_solution(13364233928450591999)
XLA Ops:
  0.6 0.0 copy-start
  0.6 1.2 %copy-done = bf16[1,1024,512]{2,1,0:T(8,128)(2,1)S(1)} copy-done((bf16[1,1024,512]{2,1,0:T(8,128)(2,1)S(1)}, bf16[1,1024,512]{2,1,0:T(8,128)(2,1)}, u32[]{:S(2)}) %copy-start) | copy-done | bytes 1048600
  1.9 0.0 copy-start.1
  1.9 0.9 %copy-done.1 = f32[512,128]{1,0:T(8,128)S(1)} copy-done((f32[512,128]{1,0:T(8,128)S(1)}, f32[512,128]{1,0:T(8,128)}, u32[]{:S(2)}) %copy-start.1) | copy-done | bytes 262168
  2.8 67.7 %step.1 = (bf16[4096,512]{1,0:T(8,128)(2,1)S(1)}, bf16[4096,512]{1,0:T(8,128)(2,1)S(1)}, bf16[4096,256]{1,0:T(8,128)(2,1)S(1)}, f32[128,512]{1,0:T(8,128)S(1)}, f32[128,512]{1,0:T(8,128)S(1)}) custom-call(bf16[1024,4096]{1,0:T(8,128)(2,1)} %bitcast.5, bf16[1024,512]{1,0:T(8,128)(2,1)S(1)} %bitcast.4, bf16[4096,512]{1,0:T(8,128)(2,1)} %bitcast.6, ...), custom_call_target="tpu_custom_call" | custom-call | tf_op jit(solution)/shard_map/step/pallas_call | solution.py:307
  70.5 4.5 %finish.1 = (bf16[4096,512]{1,0:T(8,128)(2,1)}, f32[512,128]{1,0:T(8,128)}) custom-call(bf16[4096,256]{1,0:T(8,128)(2,1)S(1)} %get-tuple-element.9.p, f32[128,512]{1,0:T(8,128)S(1)} %get-tuple-element.10.w, f32[128,512]{1,0:T(8,128)S(1)} %get-tuple-element.11.q_t, bf16[4096,512]{1,0:T(8,128)(2,1)S(1)} %get-tuple-element.12.hi, ...), custom_call_target="tpu_custom_call" | custom-call | tf_op jit(solution)/shard_map/finish/pallas_call | solution.py:385
Async XLA Ops:
  0.6 1.2 %copy-start = (bf16[1,1024,512]{2,1,0:T(8,128)(2,1)S(1)}, bf16[1,1024,512]{2,1,0:T(8,128)(2,1)}, u32[]{:S(2)}) copy-start(bf16[1,1024,512]{2,1,0:T(8,128)(2,1)} %param.5) | copy-start | bytes 3145732
  1.9 0.9 %copy-start.1 = (f32[512,128]{1,0:T(8,128)S(1)}, f32[512,128]{1,0:T(8,128)}, u32[]{:S(2)}) copy-start(f32[512,128]{1,0:T(8,128)} %q.1) | copy-start | bytes 786436

commit v3 on v0

v3 whole, which is shorter than its diff:
```python
import jax
import jax.numpy as jnp
from jax import lax
from jax.experimental import pallas as pl
from jax.experimental.pallas import tpu as pltpu
from jax.sharding import PartitionSpec as P

MESH = pl.DeviceIdType.MESH
NX, NY, NZ = 4, 4, 8
TOK, ROWS, COLS, RANK = 1024, 4096, 512, 128
CHUNKS = 4
CHUNK = ROWS // CHUNKS
SUB = CHUNK // (4 * NX * NY)
MERGE = 512
BLOCK, GROUP = 32, 16
QUARTERS = COLS // RANK
BF, F32 = jnp.bfloat16, jnp.float32
HIGHEST = lax.Precision.HIGHEST
FIRST = (((0,), (0,)), ((), ()))


def position():
    dp, mp = lax.axis_index("dp"), lax.axis_index("mp")
    return lax.rem(mp, NX), mp // NX, dp // 2, lax.rem(dp, 2)


def device(x, y, z, c):
    return (z * 2 + c, y * NX + x)


def turn(own, d, n):
    return lax.rem(own + d, n)


def remote(src, dst, send, recv, where):
    return pltpu.make_async_remote_copy(
        src_ref=src, dst_ref=dst, send_sem=send, recv_sem=recv, device_id=where, device_id_type=MESH
    )


def drain(like, sem):
    pltpu.make_async_copy(like, like, sem).wait()


def loop(first, last, body):
    def step(k, carry):
        body(k)
        return carry

    lax.fori_loop(first, last, step, 0)


def halves(value):
    high = value.astype(BF)
    return high, (value - high.astype(F32)).astype(BF)


def dot(a, b, dims=(((1,), (0,)), ((), ()))):
    return lax.dot_general(a, b, dims, preferred_element_type=F32)


def eliminate(m, b):
    at = b * BLOCK
    row = lax.broadcasted_iota(jnp.int32, (BLOCK, RANK), 0)
    sides = [m[at : at + BLOCK, :RANK], m[at : at + BLOCK, RANK:]]
    for start in range(0, BLOCK, GROUP):
        columns = [
            jnp.broadcast_to(sides[0][:, at + j : at + j + 1], (BLOCK, RANK)) for j in range(start, start + GROUP)
        ]
        for t in range(GROUP):
            j = start + t
            scale = lax.rsqrt(columns[t][j : j + 1, :])
            factor = jnp.where(row > j, columns[t] * scale, 0.0)
            for other in range(t + 1, GROUP):
                columns[other] = columns[other] - factor * factor[start + other : start + other + 1, :]
            for i in range(2):
                pivot = sides[i][j : j + 1, :] * scale
                sides[i] = jnp.where(row == j, pivot, sides[i] - factor * pivot)
    block = jnp.concatenate(sides, axis=1)
    m[at : at + BLOCK, :] = block
    if at + BLOCK < RANK:
        update = lax.dot_general(sides[0], block, FIRST, precision=HIGHEST, preferred_element_type=F32)
        m[at + BLOCK :, :] -= update[at + BLOCK :, :]


def step_kernel(
    a, g, e, q,
    hi, lo, both, w_out, q_out,
    abuf, ebuf, gbuf, qbuf, tcat, qcat, p, h, r0, r1, u, r2, zs_buf, full,
    acc, sq, cross, m, s, s0, hs, s1, sall,
    asem, esem, gsem, qsem, send, got0, got1, got2, got3, got4, bak2, bak1, bak0,
    ssend, sgot0, sgot1, sbak1, sbak0,
):
    x, y, z, c = position()
    partner = device(x, y, z, 1 - c)
    xs = [device(turn(x, d, NX), y, z, c) for d in range(1, NX)]
    ys = [device(x, turn(y, d, NY), z, c) for d in range(1, NY)]
    zs = [device(x, y, turn(z, d, NZ), c) for d in range(1, NZ)]
    rows = lambda k: pl.ds(pl.multiple_of(k * CHUNK, CHUNK), CHUNK)

    barrier = pltpu.get_barrier_semaphore()
    for peer in zs + xs + ys + [partner]:
        pl.semaphore_signal(barrier, inc=1, device_id=peer, device_id_type=MESH)

    def load_a(k):
        return pltpu.make_async_copy(a.at[:, rows(k)], abuf.at[:, rows(k)], asem.at[k])

    def load_e(k):
        return pltpu.make_async_copy(e.at[rows(k)], ebuf.at[rows(k)], esem.at[k])

    load_q = pltpu.make_async_copy(q, qbuf, qsem)
    load_g = pltpu.make_async_copy(g, gbuf, gsem)
    load_q.start()
    load_g.start()

    def load(k):
        load_a(k).start()
        load_e(k).start()

    loop(0, CHUNKS, load)
    acc[...] = jnp.zeros_like(acc)
    sq[...] = jnp.zeros_like(sq)
    cross[...] = jnp.zeros_like(cross)
    load_q.wait()
    q_high, q_low = halves(qbuf[...])
    qcat[:, :RANK] = q_high
    qcat[:, RANK:] = q_low
    load_g.wait()
    wide = dot(gbuf[...], qcat[...])
    t_high, t_low = halves(wide[:, :RANK] + wide[:, RANK:])
    tcat[:, :RANK] = t_high
    tcat[:, RANK:] = t_low

    def left(k):
        load_a(k).wait()
        load_e(k).wait()
        wide = dot(abuf[:, rows(k)], tcat[...], FIRST) + dot(ebuf[rows(k)], qcat[...])
        p[k] = (wide[:, :RANK] + wide[:, RANK:]).reshape(2, 2, NX, NY, SUB, RANK)

    def merge(n):
        part = pl.ds(pl.multiple_of(n * MERGE, MERGE), MERGE)
        high, low = halves(dot(abuf[:, part], gbuf[...], FIRST) + ebuf[part].astype(F32))
        hi[part] = high
        lo[part] = low

    def pair(k):
        remote(p.at[k, 1 - c], r0.at[k], send.at[0], got0.at[k], partner).start()

    def first(k):
        drain(r0.at[k], got0.at[k])
        h[k] = p[k, c] + r0[k]
        for d in range(1, NX):
            remote(h.at[k, 0, turn(x, d, NX)], r1.at[k, 0, d - 1], send.at[1], got1.at[k], xs[d - 1]).start()
            remote(h.at[k, 1, turn(y, d, NY)], r1.at[k, 1, d - 1], send.at[1], got1.at[k], ys[d - 1]).start()

    def second(k):
        drain(r1.at[k], got1.at[k])
        for part, own in ((0, x), (1, y)):
            u[k, part] = h[k, part, own] + r1[k, part, 0] + r1[k, part, 1] + r1[k, part, 2]
        for d in range(1, NX):
            remote(u.at[k, 0, turn(y, d, NY)], r2.at[k, 0, d - 1], send.at[2], got2.at[k], ys[d - 1]).start()
            remote(u.at[k, 1, turn(x, d, NX)], r2.at[k, 1, d - 1], send.at[2], got2.at[k], xs[d - 1]).start()

    def third(k):
        drain(r2.at[k], got2.at[k])
        for part, own in ((0, y), (1, x)):
            zs_buf[k, z, part] = u[k, part, own] + r2[k, part, 0] + r2[k, part, 1] + r2[k, part, 2]
        for d in (1, 2, NZ - 2, NZ - 1):
            remote(zs_buf.at[k, z], zs_buf.at[k, z], send.at[3], got3.at[k], zs[d - 1]).start()

    def onward(k):
        drain(zs_buf.at[k, pl.ds(0, 4)], got3.at[k])
        for part, way in ((0, 1), (1, NZ - 1)):
            origin = turn(z, NZ - 2 if way == 1 else 2, NZ)
            whole, half = zs_buf.at[k, origin], zs_buf.at[k, origin, part]
            remote(whole, whole, send.at[7], got4.at[k], zs[way - 1]).start()
            remote(half, half, send.at[7], got4.at[k], zs[(2 * way) % NZ - 1]).start()

    def second_back(k):
        drain(zs_buf.at[k, pl.ds(0, 3)], got4.at[k])
        total = zs_buf[k, 0]
        for other in range(1, NZ):
            total = total + zs_buf[k, other]
        full[k, c, 0, x, y] = total[0]
        full[k, c, 1, y, x] = total[1]
        for d in range(1, NX):
            one, two = full.at[k, c, 0, x, y], full.at[k, c, 1, y, x]
            remote(one, one, send.at[4], bak2.at[k], ys[d - 1]).start()
            remote(two, two, send.at[4], bak2.at[k], xs[d - 1]).start()

    def first_back(k):
        drain(r2.at[k], bak2.at[k])
        for d in range(1, NX):
            one, two = full.at[k, c, 0, x], full.at[k, c, 1, y]
            remote(one, one, send.at[5], bak1.at[k], xs[d - 1]).start()
            remote(two, two, send.at[5], bak1.at[k], ys[d - 1]).start()

    def pair_back(k):
        drain(r1.at[k], bak1.at[k])
        remote(full.at[k, c], full.at[k, c], send.at[6], bak0.at[k], partner).start()

    def use(k):
        drain(r0.at[k], bak0.at[k])
        block = full[k].reshape(CHUNK, RANK)
        high, low = halves(block)
        rest = ((block - high.astype(F32)) - low.astype(F32)).astype(BF)
        both[rows(k), :RANK] = high
        both[rows(k), RANK:] = low
        wide = both[rows(k)]
        acc[...] += dot(wide, hi[rows(k)], FIRST)
        acc[:RANK] += dot(high, lo[rows(k)], FIRST)
        sq[...] += dot(wide, wide, FIRST)
        cross[...] += dot(high, rest, FIRST)

    early = 3
    loop(0, early, left)
    pl.semaphore_wait(barrier, 1 + len(xs) + len(ys) + len(zs))
    loop(0, early, pair)

    def late(k):
        left(k)
        pair(k)

    loop(early, CHUNKS, late)
    ahead = 3
    loop(0, ahead, first)
    stages = (
        (second, 3, 0, CHUNKS), (first, 0, ahead, CHUNKS), (third, 5, 0, CHUNKS), (onward, 8, 0, CHUNKS),
        (second_back, 10, 0, CHUNKS), (first_back, 12, 0, CHUNKS), (pair_back, 15, 0, CHUNKS),
        (merge, 0, 0, ROWS // MERGE), (use, 16, 0, CHUNKS),
    )

    def slot(t):
        for stage, lag, start, stop in stages:
            @pl.when((t >= lag + start) & (t < lag + stop))
            def _():
                stage(t - lag)

    loop(0, stages[-1][1] + CHUNKS, slot)

    own = acc[:RANK] + acc[RANK:]
    for n in range(QUARTERS):
        s[n] = own[:, n * RANK : (n + 1) * RANK].reshape(2, NZ, 8, RANK)
        remote(s.at[n, 1 - c], s0.at[n], ssend.at[0], sgot0.at[n], partner).start()
    mixed = sq[:RANK, RANK:] + cross[...]
    m[:, :RANK] = sq[:RANK, :RANK] + (sq[RANK:, RANK:] + (mixed + mixed.T))
    diagonal = lax.broadcasted_iota(jnp.int32, (RANK, RANK), 0) == lax.broadcasted_iota(jnp.int32, (RANK, RANK), 1)
    m[:, RANK:] = diagonal.astype(F32)

    def spread(n):
        drain(s0.at[n], sgot0.at[n])
        hs[n] = s[n, c] + s0[n]
        for d in range(1, NZ):
            remote(hs.at[n, turn(z, d, NZ)], s1.at[n, d - 1], ssend.at[1], sgot1.at[n], zs[d - 1]).start()

    def gather(n):
        drain(s1.at[n], sgot1.at[n])
        total = hs[n, z]
        for d in range(NZ - 1):
            total = total + s1[n, d]
        sall[n, c, z] = total
        piece = sall.at[n, c, z]
        for d in range(1, NZ):
            remote(piece, piece, ssend.at[2], sbak1.at[n], zs[d - 1]).start()

    def share(n):
        drain(s1.at[n], sbak1.at[n])
        remote(sall.at[n, c], sall.at[n, c], ssend.at[3], sbak0.at[n], partner).start()

    def factors(ns):
        for n in ns:
            drain(s0.at[n], sbak0.at[n])
        inverse = m[:, RANK:]
        scaled = jnp.concatenate([sall[n].reshape(RANK, RANK) for n in ns], axis=1) * (1.0 / (2 * NZ))
        q_new = jnp.dot(inverse, scaled, precision=HIGHEST, preferred_element_type=F32)
        columns = slice(ns[0] * RANK, (ns[-1] + 1) * RANK)
        q_out[:, columns] = q_new
        w_out[:, columns] = lax.dot_general(inverse, q_new, FIRST, precision=HIGHEST, preferred_element_type=F32)

    eliminate(m, 0)
    loop(0, QUARTERS, spread)
    eliminate(m, 1)
    eliminate(m, 2)
    eliminate(m, 3)
    loop(0, QUARTERS, gather)
    loop(0, QUARTERS, share)
    factors((0, 1))
    factors((2, 3))

    drain(r0, send.at[0])
    drain(r1, send.at[1])
    drain(r2, send.at[2])
    drain(zs_buf.at[:, pl.ds(0, 4)], send.at[3])
    drain(zs_buf.at[:, pl.ds(0, 3)], send.at[7])
    drain(r2, send.at[4])
    drain(r1, send.at[5])
    drain(r0, send.at[6])
    drain(s0, ssend.at[0])
    drain(s1, ssend.at[1])
    drain(s1, ssend.at[2])
    drain(s0, ssend.at[3])


def step(activations, out_grads, error_fb, q_prev):
    far = pl.BlockSpec(memory_space=pltpu.HBM)
    near = pl.BlockSpec(memory_space=pltpu.VMEM)
    vm = lambda *dims: pltpu.VMEM(dims, F32)
    bf = lambda *dims: pltpu.VMEM(dims, BF)
    sem = lambda *dims: pltpu.SemaphoreType.DMA(dims)
    return pl.pallas_call(
        step_kernel,
        out_shape=[
            jax.ShapeDtypeStruct((ROWS, COLS), BF),
            jax.ShapeDtypeStruct((ROWS, COLS), BF),
            jax.ShapeDtypeStruct((ROWS, 2 * RANK), BF),
            jax.ShapeDtypeStruct((RANK, COLS), F32),
            jax.ShapeDtypeStruct((RANK, COLS), F32),
        ],
        in_specs=[far] * 4,
        out_specs=[near] * 5,
        scratch_shapes=[
            bf(TOK, ROWS),
            bf(ROWS, COLS),
            bf(TOK, COLS),
            vm(COLS, RANK),
            bf(TOK, 2 * RANK),
            bf(COLS, 2 * RANK),
            vm(CHUNKS, 2, 2, NX, NY, SUB, RANK),
            vm(CHUNKS, 2, NX, NY, SUB, RANK),
            vm(CHUNKS, 2, NX, NY, SUB, RANK),
            vm(CHUNKS, 2, NX - 1, NY, SUB, RANK),
            vm(CHUNKS, 2, NY, SUB, RANK),
            vm(CHUNKS, 2, NY - 1, SUB, RANK),
            vm(CHUNKS, NZ, 2, SUB, RANK),
            vm(CHUNKS, 2, 2, NX, NY, SUB, RANK),
            vm(2 * RANK, COLS),
            vm(2 * RANK, 2 * RANK),
            vm(RANK, RANK),
            vm(RANK, 2 * RANK),
            vm(QUARTERS, 2, NZ, 8, RANK),
            vm(QUARTERS, NZ, 8, RANK),
            vm(QUARTERS, NZ, 8, RANK),
            vm(QUARTERS, NZ - 1, 8, RANK),
            vm(QUARTERS, 2, NZ, 8, RANK),
            sem(CHUNKS),
            sem(CHUNKS),
            sem(),
            sem(),
            sem(8),
            sem(CHUNKS),
            sem(CHUNKS),
            sem(CHUNKS),
            sem(CHUNKS),
            sem(CHUNKS),
            sem(CHUNKS),
            sem(CHUNKS),
            sem(CHUNKS),
            sem(4),
            sem(QUARTERS),
            sem(QUARTERS),
            sem(QUARTERS),
            sem(QUARTERS),
        ],
        compiler_params=pltpu.CompilerParams(
            collective_id=0, has_side_effects=True, vmem_limit_bytes=40 << 20
        ),
        name="step",
    )(activations, out_grads, error_fb, q_prev)


def finish_kernel(p, w, q_t, hi, lo, out, q_new):
    @pl.when(pl.program_id(0) == 0)
    def _():
        q_new[...] = q_t[...].T

    high, low = halves(w[...])
    approx = dot(p[...], jnp.concatenate([high, high], axis=0)) + dot(p[:, :RANK], low)
    out[...] = ((hi[...].astype(F32) - approx) + lo[...].astype(F32)).astype(BF)


def finish(p, w, q_t, hi, lo):
    tile = 1024
    fixed = lambda *dims: pl.BlockSpec(dims, lambda i: (0, 0))
    moving = lambda *dims: pl.BlockSpec(dims, lambda i: (i, 0))
    return pl.pallas_call(
        finish_kernel,
        out_shape=[jax.ShapeDtypeStruct((ROWS, COLS), BF), jax.ShapeDtypeStruct((COLS, RANK), F32)],
        grid=(ROWS // tile,),
        in_specs=[
            moving(tile, 2 * RANK), fixed(RANK, COLS), fixed(RANK, COLS), moving(tile, COLS), moving(tile, COLS)
        ],
        out_specs=[moving(tile, COLS), fixed(COLS, RANK)],
        compiler_params=pltpu.CompilerParams(vmem_limit_bytes=24 << 20),
        name="finish",
    )(p, w, q_t, hi, lo)


def per_device(activations, out_grads, error_fb, q_prev):
    operands = (activations[0], out_grads[0], error_fb[0], q_prev)
    held = [pltpu.with_memory_space_constraint(each, pltpu.HBM) for each in operands]
    hi, lo, p, w, q_t = step(*held)
    new_error, q_new = finish(p, w, q_t, hi, lo)
    return (new_error[None], q_new)


def solution(mesh):
    placed = (P("dp", None, None), P("dp", None, "mp"), P("dp", None, "mp"), P("mp", None))
    return jax.shard_map(
        per_device,
        mesh=mesh,
        in_specs=placed,
        out_specs=(P("dp", None, "mp"), P("mp", None)),
        check_vma=False,
    )
```

time: 476 us -> 66.3 us (0.14)
  waiting for transfers between devices: 376 us -> 0 us
  Pallas kernels: 0 us -> 65.6 us
  matrix products: 55.1 us -> 0 us
  other arithmetic: 23.8 us -> 0 us
  between operations: 14.1 us -> 0.64 us
  local copies, waits for them, and re-layouts: 5.86 us -> 0 us
    psum x2 -> x0, waiting for transfers between devices: 376 us -> none  [the longest x1 266 us: per_device(): p_sum = lax.psum(p_local, ('dp', 'mp'))]
    pallas_call x0 -> x2, Pallas kernels: none -> 65.6 us  [the longest x1 61.2 us: step(): pl.pallas_call(step_kernel, out_shape=[jax.ShapeDtypeStruct((ROWS, COLS),...]
    dot_general x5 -> x0, matrix products: 53.3 us -> none  [the longest x1 16.2 us: per_device(): lax.dot_general(merged, p_hat, (((0,), (0,)), ((), ())), precision=lax.Pr...]
    another operation x5 -> x0, other arithmetic: 22.9 us -> none  [the longest x3 12.4 us: orthonormal(): chol = jnp.linalg.cholesky(gram)]
    unnamed x12 -> x0, local copies, waits for them, and re-layouts: 5.77 us -> none
  transfers between devices with their start and end apart: 2 -> 0, of which waited for: 2 -> 0; matrix products, arithmetic and copies ran while one was open for 0% -> 0% of each run, Pallas kernels for 0% -> 0%
where the time goes in v3:
time: 66.3 us
  Pallas kernels  65.6 us (99%)
    pallas_call x1, Pallas kernels, step(): pl.pallas_call(step_kernel, out_shape=[jax.ShapeDtypeStruct((ROWS, COLS),...  61.2 us
    pallas_call x1, Pallas kernels, finish(): pl.pallas_call(finish_kernel, out_shape=[jax.ShapeDtypeStruct((ROWS, COLS...  4.46 us

profile of v3, /device:TPU:1, one launch (start us, length us, event | category | flops | bytes accessed | tf_op | source)
XLA Modules:
  0.0 66.3 jit_solution(16526181035176122102)
XLA Ops:
  0.6 61.2 %step.1 = (bf16[4096,512]{1,0:T(8,128)(2,1)S(1)}, bf16[4096,512]{1,0:T(8,128)(2,1)S(1)}, bf16[4096,256]{1,0:T(8,128)(2,1)S(1)}, f32[128,512]{1,0:T(8,128)S(1)}, f32[128,512]{1,0:T(8,128)S(1)}) custom-call(bf16[1024,4096]{1,0:T(8,128)(2,1)} %bitcast.4, bf16[1024,512]{1,0:T(8,128)(2,1)} %bitcast.6, bf16[4096,512]{1,0:T(8,128)(2,1)} %bitcast.5, f32[512,128]{1,0:T(8,128)} %q.1), custom_call_target="tpu_custom_call" | custom-call | tf_op jit(solution)/shard_map/step/pallas_call | solution.py:310
  61.8 4.5 %finish.1 = (bf16[4096,512]{1,0:T(8,128)(2,1)}, f32[512,128]{1,0:T(8,128)}) custom-call(bf16[4096,256]{1,0:T(8,128)(2,1)S(1)} %get-tuple-element.9.p, f32[128,512]{1,0:T(8,128)S(1)} %get-tuple-element.10.w, f32[128,512]{1,0:T(8,128)S(1)} %get-tuple-element.11.q_t, bf16[4096,512]{1,0:T(8,128)(2,1)S(1)} %get-tuple-element.12.hi, ...), custom_call_target="tpu_custom_call" | custom-call | tf_op jit(solution)/shard_map/finish/pallas_call | solution.py:385

commit v4 on v3

--- a/solution.py
+++ b/solution.py
@@ -199,18 +199,25 @@
         drain(r1.at[k], bak1.at[k])
         remote(full.at[k, c], full.at[k, c], send.at[6], bak0.at[k], partner).start()
 
-    def use(k):
-        drain(r0.at[k], bak0.at[k])
-        block = full[k].reshape(CHUNK, RANK)
+    def use(k, half):
+        block = full[k, half].reshape(CHUNK // 2, RANK)
+        part = pl.ds(pl.multiple_of(k * CHUNK + half * (CHUNK // 2), CHUNK // 2), CHUNK // 2)
         high, low = halves(block)
         rest = ((block - high.astype(F32)) - low.astype(F32)).astype(BF)
-        both[rows(k), :RANK] = high
-        both[rows(k), RANK:] = low
-        wide = both[rows(k)]
-        acc[...] += dot(wide, hi[rows(k)], FIRST)
-        acc[:RANK] += dot(high, lo[rows(k)], FIRST)
+        both[part, :RANK] = high
+        both[part, RANK:] = low
+        wide = both[part]
+        acc[...] += dot(wide, hi[part], FIRST)
+        acc[:RANK] += dot(high, lo[part], FIRST)
         sq[...] += dot(wide, wide, FIRST)
         cross[...] += dot(high, rest, FIRST)
+
+    def use_own(k):
+        use(k, c)
+
+    def use_other(k):
+        drain(r0.at[k], bak0.at[k])
+        use(k, 1 - c)
 
     early = 3
     loop(0, early, left)
@@ -227,7 +234,7 @@
     stages = (
         (second, 3, 0, CHUNKS), (first, 0, ahead, CHUNKS), (third, 5, 0, CHUNKS), (onward, 8, 0, CHUNKS),
         (second_back, 10, 0, CHUNKS), (first_back, 12, 0, CHUNKS), (pair_back, 15, 0, CHUNKS),
-        (merge, 0, 0, ROWS // MERGE), (use, 16, 0, CHUNKS),
+        (merge, 0, 0, ROWS // MERGE), (use_own, 15, 0, CHUNKS), (use_other, 16, 0, CHUNKS),
     )
 
     def slot(t):
@@ -270,12 +277,11 @@
     def factors(ns):
         for n in ns:
             drain(s0.at[n], sbak0.at[n])
-        inverse = m[:, RANK:]
         scaled = jnp.concatenate([sall[n].reshape(RANK, RANK) for n in ns], axis=1) * (1.0 / (2 * NZ))
-        q_new = jnp.dot(inverse, scaled, precision=HIGHEST, preferred_element_type=F32)
+        q_new = jnp.dot(m[:, RANK:], scaled, precision=HIGHEST, preferred_element_type=F32)
         columns = slice(ns[0] * RANK, (ns[-1] + 1) * RANK)
         q_out[:, columns] = q_new
-        w_out[:, columns] = lax.dot_general(inverse, q_new, FIRST, precision=HIGHEST, preferred_element_type=F32)
+        w_out[:, columns] = lax.dot_general(m[:, RANK:], q_new, FIRST, precision=HIGHEST, preferred_element_type=F32)
 
     eliminate(m, 0)
     loop(0, QUARTERS, spread)

time: 66.3 us -> 66.3 us (level)
  no operation moved by 1% of the time
where the time goes in v4:
time: 66.3 us
  Pallas kernels  65.6 us (99%)
    pallas_call x1, Pallas kernels, step(): pl.pallas_call(step_kernel, out_shape=[jax.ShapeDtypeStruct((ROWS, COLS),...  61.2 us
    pallas_call x1, Pallas kernels, finish(): pl.pallas_call(finish_kernel, out_shape=[jax.ShapeDtypeStruct((ROWS, COLS...  4.46 us

profile of v4, /device:TPU:1, one launch (start us, length us, event | category | flops | bytes accessed | tf_op | source)
XLA Modules:
  0.0 66.3 jit_solution(2092945442630811899)
XLA Ops:
  0.6 61.2 %step.1 = (bf16[4096,512]{1,0:T(8,128)(2,1)S(1)}, bf16[4096,512]{1,0:T(8,128)(2,1)S(1)}, bf16[4096,256]{1,0:T(8,128)(2,1)S(1)}, f32[128,512]{1,0:T(8,128)S(1)}, f32[128,512]{1,0:T(8,128)S(1)}) custom-call(bf16[1024,4096]{1,0:T(8,128)(2,1)} %bitcast.4, bf16[1024,512]{1,0:T(8,128)(2,1)} %bitcast.6, bf16[4096,512]{1,0:T(8,128)(2,1)} %bitcast.5, f32[512,128]{1,0:T(8,128)} %q.1), custom_call_target="tpu_custom_call" | custom-call | tf_op jit(solution)/shard_map/step/pallas_call | solution.py:316
  61.8 4.5 %finish.1 = (bf16[4096,512]{1,0:T(8,128)(2,1)}, f32[512,128]{1,0:T(8,128)}) custom-call(bf16[4096,256]{1,0:T(8,128)(2,1)S(1)} %get-tuple-element.9.p, f32[128,512]{1,0:T(8,128)S(1)} %get-tuple-element.10.w, f32[128,512]{1,0:T(8,128)S(1)} %get-tuple-element.11.q_t, bf16[4096,512]{1,0:T(8,128)(2,1)S(1)} %get-tuple-element.12.hi, ...), custom_call_target="tpu_custom_call" | custom-call | tf_op jit(solution)/shard_map/finish/pallas_call | solution.py:391

commit v5 on v4

--- a/solution.py
+++ b/solution.py
@@ -12,6 +12,7 @@
 CHUNK = ROWS // CHUNKS
 SUB = CHUNK // (4 * NX * NY)
 MERGE = 512
+TILE = 512
 BLOCK, GROUP = 32, 16
 QUARTERS = COLS // RANK
 BF, F32 = jnp.bfloat16, jnp.float32
@@ -374,28 +375,34 @@
     )(activations, out_grads, error_fb, q_prev)
 
 
-def finish_kernel(p, w, q_t, hi, lo, out, q_new):
-    @pl.when(pl.program_id(0) == 0)
-    def _():
-        q_new[...] = q_t[...].T
-
+def finish_kernel(p, w, q_t, hi, lo, out, q_new, weights, ready, sem):
     high, low = halves(w[...])
-    approx = dot(p[...], jnp.concatenate([high, high], axis=0)) + dot(p[:, :RANK], low)
-    out[...] = ((hi[...].astype(F32) - approx) + lo[...].astype(F32)).astype(BF)
+    weights[:RANK] = high
+    weights[RANK : 2 * RANK] = high
+    weights[2 * RANK :] = low
+
+    def tile(k):
+        part = slice(k * TILE, (k + 1) * TILE)
+        approx = dot(p[part], weights[: 2 * RANK]) + dot(p[part, :RANK], weights[2 * RANK :])
+        ready[part] = ((hi[part].astype(F32) - approx) + lo[part].astype(F32)).astype(BF)
+        pltpu.make_async_copy(ready.at[part], out.at[part], sem).start()
+
+    for k in range(ROWS // TILE):
+        tile(k)
+    q_new[...] = q_t[...].T
+    pltpu.make_async_copy(ready, out, sem).wait()
 
 
 def finish(p, w, q_t, hi, lo):
-    tile = 1024
-    fixed = lambda *dims: pl.BlockSpec(dims, lambda i: (0, 0))
-    moving = lambda *dims: pl.BlockSpec(dims, lambda i: (i, 0))
+    near = pl.BlockSpec(memory_space=pltpu.VMEM)
     return pl.pallas_call(
         finish_kernel,
         out_shape=[jax.ShapeDtypeStruct((ROWS, COLS), BF), jax.ShapeDtypeStruct((COLS, RANK), F32)],
-        grid=(ROWS // tile,),
-        in_specs=[
-            moving(tile, 2 * RANK), fixed(RANK, COLS), fixed(RANK, COLS), moving(tile, COLS), moving(tile, COLS)
+        in_specs=[near] * 5,
+        out_specs=[pl.BlockSpec(memory_space=pltpu.HBM), near],
+        scratch_shapes=[
+            pltpu.VMEM((3 * RANK, COLS), BF), pltpu.VMEM((ROWS, COLS), BF), pltpu.SemaphoreType.DMA(())
         ],
-        out_specs=[moving(tile, COLS), fixed(COLS, RANK)],
         compiler_params=pltpu.CompilerParams(vmem_limit_bytes=24 << 20),
         name="finish",
     )(p, w, q_t, hi, lo)

time: 66.3 us -> 66 us (level)
  no operation moved by 1% of the time
where the time goes in v5:
time: 66 us; the launch traced here: 65.9 us
  Pallas kernels  65.3 us (99%)
    pallas_call x1, Pallas kernels, step(): pl.pallas_call(step_kernel, out_shape=[jax.ShapeDtypeStruct((ROWS, COLS),...  61.2 us
    pallas_call x1, Pallas kernels, finish(): pl.pallas_call(finish_kernel, out_shape=[jax.ShapeDtypeStruct((ROWS, COLS...  4.11 us

profile of v5, /device:TPU:1, one launch (start us, length us, event | category | flops | bytes accessed | tf_op | source)
XLA Modules:
  0.0 65.9 jit_solution(4692617386883715947)
XLA Ops:
  0.6 61.2 %step.1 = (bf16[4096,512]{1,0:T(8,128)(2,1)S(1)}, bf16[4096,512]{1,0:T(8,128)(2,1)S(1)}, bf16[4096,256]{1,0:T(8,128)(2,1)S(1)}, f32[128,512]{1,0:T(8,128)S(1)}, f32[128,512]{1,0:T(8,128)S(1)}) custom-call(bf16[1024,4096]{1,0:T(8,128)(2,1)} %bitcast.4, bf16[1024,512]{1,0:T(8,128)(2,1)} %bitcast.6, bf16[4096,512]{1,0:T(8,128)(2,1)} %bitcast.5, f32[512,128]{1,0:T(8,128)} %q.1), custom_call_target="tpu_custom_call" | custom-call | tf_op jit(solution)/shard_map/step/pallas_call | solution.py:317
  61.8 4.1 %finish.1 = (bf16[4096,512]{1,0:T(8,128)(2,1)}, f32[512,128]{1,0:T(8,128)}) custom-call(bf16[4096,256]{1,0:T(8,128)(2,1)S(1)} %get-tuple-element.9.p, f32[128,512]{1,0:T(8,128)S(1)} %get-tuple-element.10.w, f32[128,512]{1,0:T(8,128)S(1)} %get-tuple-element.11.q_t, bf16[4096,512]{1,0:T(8,128)(2,1)S(1)} %get-tuple-element.12.hi, ...), custom_call_target="tpu_custom_call" | custom-call | tf_op jit(solution)/shard_map/finish/pallas_call | solution.py:398
